TPU v7x, 32 devices: a whole 2x2x4 slice. The times are simulated.
32 devices in a mesh: groups: 2 (over y), width: 4 (over z), hidden: 4 (over x, core).
Axes of the slice: x: 2, y: 2, z: 4, core: 2. Of those that a mesh axis runs over, the one named last changes fastest.
Arguments:
- inputs: bfloat16 [2, 16, 8192], P(None, 'groups', 'width'), parts along dimension 1, may hold values from -6 to 6
- attn_gain: float32 [8192], P('width'), may hold values from 0.5 to 2
- w_query: bfloat16 [8192, 8192], P('width', 'hidden'), may hold values from -0.0625 to 0.0625
- w_key: bfloat16 [8192, 1024], P('width', 'hidden'), may hold values from -0.0625 to 0.0625
- w_value: bfloat16 [8192, 1024], P('width', 'hidden'), may hold values from -0.0625 to 0.0625
- w_out: bfloat16 [8192, 8192], P('hidden', 'width'), may hold values from -0.0625 to 0.0625
- ffn_gain: float32 [8192], P('width'), may hold values from 0.5 to 2
- w_gate: bfloat16 [8192, 14336], P('width', 'hidden'), may hold values from -0.0625 to 0.0625
- w_up: bfloat16 [8192, 14336], P('width', 'hidden'), may hold values from -0.0625 to 0.0625
- w_down: bfloat16 [14336, 8192], P('hidden', 'width'), may hold values from -0.046875 to 0.046875
- key_cache: bfloat16 [16, 8, 2048, 128], P(('groups', 'width'), 'hidden'), parts along dimension 0
- value_cache: bfloat16 [16, 8, 2048, 128], P(('groups', 'width'), 'hidden'), parts along dimension 0, may hold values from -6 to 6
- lengths: int32 [16], P(('groups', 'width')), parts along dimension 0, may hold values from 1 to 2046, as said below
- positions: int32 [16], P(('groups', 'width')), parts along dimension 0, may hold values from 0 to 8191
Outputs:
- outputs: bfloat16 [2, 16, 8192], P(None, 'groups', 'width'), parts along dimension 1
There are 2 independent parts, one for each index of `groups`. A program takes and returns all parts, laid end to end along the dimension named above; an argument that names none is the same for every part. Nothing has to cross between parts.
Inputs may be any that keep to these rules, and one draw needn't show every extreme that they name: `lengths`: some request has exactly 2046 filled slots and some has exactly one.
All inputs are finite; a program needn't handle non-finite values.
Results may differ from a plain program's by a relative error of at most 0.0082.
Values may be sent and summed in bfloat16 or wider, within the bound.
A program may use at most 128 MiB of HBM per device.

v0:
```python
import functools
import math

import jax
import jax.numpy as jnp
import numpy as np
from jax import lax
from jax.experimental import pallas as pl
from jax.experimental.pallas import tpu as pltpu
from jax.sharding import PartitionSpec as P

HD = 128


def rotary(vectors, places):
    half_dim = vectors.shape[-1] // 2
    freqs = 500000.0 ** (-(jnp.arange(half_dim, dtype=jnp.float32) * 2.0 / vectors.shape[-1]))
    angles = places.astype(jnp.float32)[:, None, None] * freqs
    cosine = jnp.cos(angles)
    sine_vals = jnp.sin(angles)
    first_half = vectors[..., :half_dim]
    second_half = vectors[..., half_dim:]
    return jnp.concatenate(
        [
            first_half * cosine - second_half * sine_vals,
            second_half * cosine + first_half * sine_vals,
        ],
        axis=-1,
    )


def attention(queries, keys, values, new_keys, new_values, lengths):
    rows, steps = queries.shape[:2]
    kv_count = keys.shape[1]
    grouped = queries.reshape(rows, steps, kv_count, -1, HD)
    scale = 1.0 / math.sqrt(HD)
    old = jnp.einsum("rskgd,rkcd->rksgc", grouped, keys, preferred_element_type=jnp.float32) * scale
    new = (
        jnp.einsum("rskgd,rtkd->rksgt", grouped, new_keys, preferred_element_type=jnp.float32)
        * scale
    )
    seen = jnp.arange(keys.shape[2], dtype=jnp.int32) < lengths[:, None]
    seen = seen[:, None, None, None, :]
    order = jnp.arange(steps)[None, :] <= jnp.arange(steps)[:, None]
    order = order[None, None, :, None, :]
    old = jnp.where(seen, old, -1e30)
    new = jnp.where(order, new, -1e30)
    highest = jnp.maximum(jnp.max(old, axis=-1, keepdims=True), jnp.max(new, axis=-1, keepdims=True))
    old = jnp.where(seen, jnp.exp(old - highest), 0.0)
    new = jnp.where(order, jnp.exp(new - highest), 0.0)
    total = jnp.sum(old, axis=-1, keepdims=True) + jnp.sum(new, axis=-1, keepdims=True)
    old = (old / total).astype(jnp.bfloat16)
    new = (new / total).astype(jnp.bfloat16)
    mixed = jnp.einsum("rksgc,rkcd->rskgd", old, values, preferred_element_type=jnp.float32)
    mixed += jnp.einsum("rksgt,rtkd->rskgd", new, new_values, preferred_element_type=jnp.float32)
    return mixed.astype(jnp.bfloat16).reshape(rows, steps, -1)


def plain(
    inputs,
    attn_gain,
    w_query,
    w_key,
    w_value,
    w_out,
    ffn_gain,
    w_gate,
    w_up,
    w_down,
    key_cache,
    value_cache,
    lengths,
    positions,
):
    local_rows = key_cache.shape[0]
    steps, requests, depth = inputs.shape
    width = requests // local_rows * depth
    query_cols = w_query.shape[1]
    key_cols = w_key.shape[1]
    hidden_cols = w_gate.shape[1]
    rows = requests * steps
    current = inputs.transpose(1, 0, 2).reshape(rows, depth).astype(jnp.float32)
    squares = jnp.sum(current * current, axis=1, keepdims=True)
    scaled = (current * attn_gain).astype(jnp.bfloat16)
    joined = lax.psum_scatter(
        jnp.concatenate(
            [
                jnp.dot(scaled, w_query, preferred_element_type=jnp.float32),
                jnp.dot(scaled, w_key, preferred_element_type=jnp.float32),
                jnp.dot(scaled, w_value, preferred_element_type=jnp.float32),
                jnp.broadcast_to(squares, (rows, 128)),
            ],
            axis=1,
        ),
        "width",
        scatter_dimension=0,
        tiled=True,
    )
    inverse = lax.rsqrt(joined[:, -1:] / width + 1e-05)
    joined = joined * inverse
    shape = (local_rows * steps, -1, HD)
    places = (positions[:, None] + jnp.arange(steps, dtype=jnp.int32)).reshape(-1)
    turned = rotary(joined[:, : query_cols + key_cols].reshape(shape), places).astype(jnp.bfloat16)
    queries = turned[:, : query_cols // HD].reshape(local_rows, steps, -1, HD)
    new_keys = turned[:, query_cols // HD :].reshape(local_rows, steps, -1, HD)
    new_values = joined[:, query_cols + key_cols : query_cols + 2 * key_cols]
    new_values = new_values.astype(jnp.bfloat16).reshape(local_rows, steps, -1, HD)
    mixed = attention(queries, key_cache, value_cache, new_keys, new_values, lengths)
    attn_part = jnp.dot(
        lax.all_gather(mixed.reshape(local_rows * steps, -1), "width", axis=0, tiled=True),
        w_out,
        preferred_element_type=jnp.float32,
    )
    residual = current + lax.psum(attn_part, "hidden")
    res_squares = jnp.sum(residual * residual, axis=1, keepdims=True)
    ffn_in = (residual * ffn_gain).astype(jnp.bfloat16)
    both = lax.psum(
        jnp.concatenate(
            [
                jnp.dot(ffn_in, w_gate, preferred_element_type=jnp.float32),
                jnp.dot(ffn_in, w_up, preferred_element_type=jnp.float32),
                jnp.broadcast_to(res_squares, (rows, 128)),
            ],
            axis=1,
        ),
        "width",
    )
    summed = both * lax.rsqrt(both[:, -1:] / width + 1e-05)
    activated = (
        jax.nn.silu(summed[:, :hidden_cols]) * summed[:, hidden_cols : 2 * hidden_cols]
    ).astype(jnp.bfloat16)
    down_part = jnp.dot(activated, w_down, preferred_element_type=jnp.float32)
    total = lax.psum(down_part, "hidden")
    out = (residual + total).astype(jnp.bfloat16)
    return out.reshape(requests, steps, depth).transpose(1, 0, 2)


MESH = pl.DeviceIdType.MESH


def layer_kernel(
    wide,
    deep,
    lengths,
    positions,
    x_hbm,
    attn_gain_hbm,
    ffn_gain_hbm,
    perm_hbm,
    unperm_hbm,
    freqs_hbm,
    w_query,
    w_key,
    w_value,
    w_out,
    w_gate,
    w_up,
    w_down,
    key_cache,
    value_cache,
    out_ref,
    x_ref,
    attn_gain,
    ffn_gain,
    perm,
    unperm,
    freqs,
    angle_buf,
    down_buf,
    wq_buf,
    wkv_buf,
    wo_buf,
    wg_buf,
    wu_buf,
    kc_buf,
    vc_buf,
    send1,
    recv1,
    ss_send1,
    ss_recv1,
    q_buf,
    k_buf,
    v_buf,
    mix_buf,
    gather,
    red1,
    res_buf,
    send3,
    recv3,
    ss2,
    act_buf,
    red2,
    load_sem,
    small_sem,
    big_sem,
    down_sem,
    s1,
    r1,
    t1,
    u1,
    s2,
    r2,
    s3,
    r3,
    s4,
    r4,
    t4,
    u4,
    s5,
    r5,
    s6,
    r6,
):
    f32, bf16 = jnp.float32, jnp.bfloat16
    col = lax.axis_index("width")
    hid = lax.axis_index("hidden")
    steps, requests, depth = x_ref.shape
    rows = steps * requests
    local_rows, kv_count, slots, _ = kc_buf.shape
    own = steps * local_rows
    query_cols = wq_buf.shape[1]
    key_cols = w_key.shape[1]
    group = query_cols // key_cols
    part = wg_buf.shape[2]
    chunks, tile = red1.shape[1], red1.shape[3]
    width = wide * depth
    far = sorted(range(1, wide), key=lambda k: abs(k - wide // 2))

    def peer(base, k, n):
        return lax.rem(base + k, n)

    def dot(a, b):
        return jnp.dot(a, b, preferred_element_type=f32)

    barrier = pltpu.get_barrier_semaphore()
    for k in range(1, wide):
        pl.semaphore_signal(
            barrier, inc=1, device_id={"width": peer(col, k, wide)}, device_id_type=MESH
        )
    for k in range(1, deep):
        pl.semaphore_signal(
            barrier, inc=1, device_id={"hidden": peer(hid, k, deep)}, device_id_type=MESH
        )

    smalls = [
        pltpu.make_async_copy(src, dst, small_sem.at[i])
        for i, (src, dst) in enumerate(
            (
                (x_hbm, x_ref),
                (perm_hbm, perm),
                (attn_gain_hbm, attn_gain),
                (freqs_hbm, freqs),
                (unperm_hbm, unperm),
                (ffn_gain_hbm, ffn_gain),
            )
        )
    ]
    for load in smalls:
        load.start()
    loads = [
        pltpu.make_async_copy(w_key, wkv_buf.at[0], load_sem.at[0]),
        pltpu.make_async_copy(w_value, wkv_buf.at[1], load_sem.at[1]),
    ]
    pieces = send1.shape[0] - 1
    q_tile = query_cols // pieces
    for c in range(pieces):
        at = pl.ds(c * q_tile, q_tile)
        loads.append(
            pltpu.make_async_copy(w_query.at[:, at], wq_buf.at[:, at], load_sem.at[2 + c])
        )
    key_load = pltpu.make_async_copy(key_cache, kc_buf, load_sem.at[2 + pieces])
    value_load = pltpu.make_async_copy(value_cache, vc_buf, load_sem.at[3 + pieces])
    out_load = pltpu.make_async_copy(w_out, wo_buf, load_sem.at[4 + pieces])
    for load in loads:
        load.start()
    for load in smalls[:4]:
        load.wait()
    order = far + [0]
    big = {}
    for k in order:
        at = pl.ds(pl.multiple_of(peer(col, k, wide) * part, 128), part)
        big[k] = (
            pltpu.make_async_copy(w_gate.at[:, at], wg_buf.at[k], big_sem.at[0, k]),
            pltpu.make_async_copy(w_up.at[:, at], wu_buf.at[k], big_sem.at[1, k]),
        )
    down_loads = {}
    for i, k in enumerate([0] + far[::-1]):
        at = pl.ds(pl.multiple_of(peer(col + wide, -k, wide) * part, 128), part)
        home = wq_buf if i < wide // 2 else wo_buf
        place = pl.ds(i % (wide // 2) * part, part)
        down_loads[k] = (
            pltpu.make_async_copy(w_down.at[at], home.at[place], down_sem.at[k]),
            home,
            i % (wide // 2) * part,
        )

    x_bf = jnp.concatenate([x_ref[s].astype(f32) for s in range(steps)], axis=0)
    turned = dot(perm[...], x_bf.astype(bf16))
    squares = jnp.sum(turned * turned, axis=1, keepdims=True)
    squares = jnp.broadcast_to(squares, (rows, 128))
    scaled = (turned * attn_gain[...]).astype(bf16)
    for w in range(wide):
        ss_send1[w] = squares[w * own : (w + 1) * own]

    first = []

    def put(value, piece):
        value = value.astype(bf16)
        for w in range(wide):
            send1[piece, w] = value[w * own : (w + 1) * own]

    def ship(src, dst, a, b):
        for k in far:
            to = peer(col, k, wide)
            copy = pltpu.make_async_remote_copy(
                src_ref=src.at[to],
                dst_ref=dst.at[k],
                send_sem=a.at[k],
                recv_sem=b.at[k],
                device_id={"width": to},
                device_id_type=MESH,
            )
            copy.start()
            first.append(copy)

    for r in range(local_rows):
        for s in range(steps):
            place = (positions[r] + s).astype(f32)
            angle_buf[0, r, s * group : (s + 1) * group, :] = jnp.broadcast_to(
                place * freqs[...], (group, HD)
            )
    angles = [angle_buf[0, r] for r in range(local_rows)]
    lower_half = lax.broadcasted_iota(jnp.int32, (steps * group, HD), 1) < HD // 2
    for r in range(local_rows):
        sin = jnp.sin(angles[r])
        angle_buf[0, r] = jnp.cos(angles[r])
        angle_buf[1, r] = jnp.where(lower_half, -sin, sin)
    loads[0].wait()
    loads[1].wait()
    put(jnp.concatenate([dot(scaled, wkv_buf[0]), dot(scaled, wkv_buf[1])], axis=1), 0)
    pl.semaphore_wait(barrier, wide + deep - 2)
    ship(ss_send1, ss_recv1, t1, u1)
    ship(send1.at[0], recv1.at[0], s1.at[0], r1.at[0])
    for c in range(pieces):
        loads[2 + c].wait()
        if c == 0:
            key_load.start()
            value_load.start()
        if c == 1:
            out_load.start()
        if 2 <= c < 2 + wide:
            for load in big[order[c - 2]]:
                load.start()
        put(dot(scaled, wq_buf[:, c * q_tile : (c + 1) * q_tile]), c + 1)
        ship(send1.at[c + 1], recv1.at[c + 1], s1.at[c + 1], r1.at[c + 1])
    for k in order[max(0, pieces - 2) :]:
        for load in big[k]:
            load.start()
    for k in [0] + far[::-1]:
        if down_loads[k][1] is wq_buf:
            down_loads[k][0].start()
    for copy in first:
        copy.wait_recv()
    sums = ss_send1[col]
    for k in range(1, wide):
        sums += ss_recv1[k]
    inverse = lax.rsqrt(sums[:, :1] / width + 1e-05)
    totals = []
    for piece in range(pieces + 1):
        value = send1[piece, col].astype(f32)
        for k in range(1, wide):
            value += recv1[piece, k].astype(f32)
        totals.append(value * inverse)
    total = jnp.concatenate(totals[1:] + totals[:1], axis=1)

    for r in range(local_rows):
        for h in range(kv_count):
            for s in range(steps):
                row = r * steps + s
                line = total[row : row + 1]
                for g in range(group):
                    at = (h * group + g) * HD
                    q_buf[r * kv_count + h, s * group + g : s * group + g + 1, :] = line[
                        :, at : at + HD
                    ]
                at = query_cols + h * HD
                k_buf[r * kv_count + h, s * group : (s + 1) * group, :] = jnp.broadcast_to(
                    line[:, at : at + HD], (group, HD)
                )
                at += key_cols
                v_buf[r * kv_count + h, s * group : (s + 1) * group, :] = jnp.broadcast_to(
                    line[:, at : at + HD], (group, HD)
                )
    key_load.wait()
    value_load.wait()
    second = []
    scale = 1.0 / math.sqrt(HD)
    step_of = lax.broadcasted_iota(jnp.int32, (steps * group, 1), 0)
    slot = lax.broadcasted_iota(jnp.int32, (steps * group, slots), 1)
    for r in range(local_rows):
        cos, sin = angle_buf[0, r], angle_buf[1, r]
        seen = slot < lengths[r]
        for h in range(kv_count):
            q = q_buf[r * kv_count + h]
            q = (q * cos + pltpu.roll(q, HD // 2, 1) * sin).astype(bf16)
            nk = k_buf[r * kv_count + h]
            nk = (nk * cos + pltpu.roll(nk, HD // 2, 1) * sin).astype(bf16).astype(f32)
            nv = v_buf[r * kv_count + h].astype(bf16).astype(f32)
            scores = lax.dot_general(
                q, kc_buf[r, h], (((1,), (1,)), ((), ())), preferred_element_type=f32
            )
            scores = jnp.where(seen, scores * scale, -1e30)
            highest = jnp.max(scores, axis=1, keepdims=True)
            fresh = []
            for s in range(steps):
                new = jnp.sum(q.astype(f32) * nk[s * group : s * group + 1], axis=1, keepdims=True)
                new = jnp.where(step_of >= s * group, new * scale, -1e30)
                fresh.append(new)
                highest = jnp.maximum(highest, new)
            weights = jnp.where(seen, jnp.exp(scores - highest), 0.0)
            norm = jnp.sum(weights, axis=1, keepdims=True)
            for s in range(steps):
                fresh[s] = jnp.where(step_of >= s * group, jnp.exp(fresh[s] - highest), 0.0)
                norm += fresh[s]
            inverse = 1.0 / norm
            mixed = dot((weights * inverse).astype(bf16), vc_buf[r, h])
            for s in range(steps):
                prob = (fresh[s] * inverse).astype(bf16).astype(f32)
                mixed += prob * nv[s * group : s * group + 1]
            for s in range(steps):
                for g in range(group):
                    at = (h * group + g) * HD
                    mix_buf[r, s : s + 1, at : at + HD] = mixed[s * group + g : s * group + g + 1]
        gather[col, r] = mix_buf[r].astype(bf16)
        for k in far:
            copy = pltpu.make_async_remote_copy(
                src_ref=gather.at[col, r],
                dst_ref=gather.at[col, r],
                send_sem=s2.at[r, k],
                recv_sem=r2.at[r, k],
                device_id={"width": peer(col, k, wide)},
                device_id_type=MESH,
            )
            copy.start()
            second.append(copy)
    for load in smalls[4:]:
        load.wait()
    for copy in second:
        copy.wait_recv()
    mixed = jnp.concatenate([gather[w, r].astype(f32) for w in range(wide) for r in range(local_rows)], axis=0).astype(bf16)
    mixed = dot(unperm[...], mixed).astype(bf16)

    def spread(red, c, a, b):
        copies = []
        for k in range(deep - 1, 0, -1):
            copy = pltpu.make_async_remote_copy(
                src_ref=red.at[hid, c],
                dst_ref=red.at[hid, c],
                send_sem=a.at[c, k],
                recv_sem=b.at[c, k],
                device_id={"hidden": peer(hid, k, deep)},
                device_id_type=MESH,
            )
            copy.start()
            copies.append(copy)
        return copies

    out_load.wait()
    third = []
    for c in range(chunks):
        red1[hid, c] = dot(mixed, wo_buf[:, c * tile : (c + 1) * tile]).astype(bf16)
        third.append(spread(red1, c, s3, r3))
    for k in [0] + far[::-1]:
        if down_loads[k][1] is wo_buf:
            down_loads[k][0].start()
    res_squares = jnp.zeros((rows, 1), f32)
    for c in range(chunks):
        for copy in third[c]:
            copy.wait_recv()
        at = slice(c * tile, (c + 1) * tile)
        value = red1[0, c].astype(f32)
        for i in range(1, deep):
            value += red1[i, c].astype(f32)
        value += jnp.concatenate([x_ref[s, :, at].astype(f32) for s in range(steps)], axis=0)
        res_buf[:, at] = value
        res_squares += jnp.sum(value * value, axis=1, keepdims=True)
    ss2[col] = jnp.broadcast_to(res_squares, (rows, 128))
    fourth = []
    for k in far:
        copy = pltpu.make_async_remote_copy(
            src_ref=ss2.at[col],
            dst_ref=ss2.at[col],
            send_sem=t4.at[k],
            recv_sem=u4.at[k],
            device_id={"width": peer(col, k, wide)},
            device_id_type=MESH,
        )
        copy.start()
        fourth.append(copy)

    ffn_in = (res_buf[...] * ffn_gain[...]).astype(bf16)
    for k in order:
        big[k][0].wait()
        send3[k, 0] = dot(ffn_in, wg_buf[k]).astype(bf16)
        big[k][1].wait()
        send3[k, 1] = dot(ffn_in, wu_buf[k]).astype(bf16)
        if k:
            copy = pltpu.make_async_remote_copy(
                src_ref=send3.at[k],
                dst_ref=recv3.at[k],
                send_sem=s4.at[k],
                recv_sem=r4.at[k],
                device_id={"width": peer(col, k, wide)},
                device_id_type=MESH,
            )
            copy.start()
            fourth.append(copy)
    gate, up = send3[0, 0].astype(f32), send3[0, 1].astype(f32)
    for copy in fourth:
        copy.wait_recv()
    sums = ss2[0]
    for w in range(1, wide):
        sums += ss2[w]
    for k in range(1, wide):
        gate += recv3[k, 0].astype(f32)
        up += recv3[k, 1].astype(f32)
    inverse = lax.rsqrt(sums[:, :1] / width + 1e-05)
    gate, up = gate * inverse, up * inverse
    act_buf[col] = (gate / (1.0 + jnp.exp(-gate)) * up).astype(bf16)
    fifth = {}
    for k in far:
        fifth[k] = pltpu.make_async_remote_copy(
            src_ref=act_buf.at[col],
            dst_ref=act_buf.at[col],
            send_sem=s5.at[k],
            recv_sem=r5.at[k],
            device_id={"width": peer(col, k, wide)},
            device_id_type=MESH,
        )
        fifth[k].start()
    sources = [0] + far[::-1]
    for k in sources:
        down_loads[k][0].wait()
    for k in sources[:-1]:
        if k:
            fifth[k].wait_recv()
        act = act_buf[peer(col + wide, -k, wide)]
        _, home, at = down_loads[k]
        for c in range(chunks):
            cut = slice(c * tile, (c + 1) * tile)
            value = dot(act, home[at : at + part, cut])
            down_buf[:, cut] = value if k == 0 else down_buf[:, cut] + value
    k = sources[-1]
    fifth[k].wait_recv()
    act = act_buf[peer(col + wide, -k, wide)]
    _, home, at = down_loads[k]
    sixth = []
    for c in range(chunks):
        cut = slice(c * tile, (c + 1) * tile)
        value = down_buf[:, cut] + dot(act, home[at : at + part, cut])
        red2[hid, c] = value.astype(bf16)
        sixth.append(spread(red2, c, s6, r6))
    for c in range(chunks):
        for copy in sixth[c]:
            copy.wait_recv()
        at = slice(c * tile, (c + 1) * tile)
        value = red2[0, c].astype(f32)
        for i in range(1, deep):
            value += red2[i, c].astype(f32)
        value = res_buf[:, at] + value
        for s in range(steps):
            out_ref[s, :, at] = value[s * requests : (s + 1) * requests]
    for copies in [first, second, fourth, list(fifth.values())] + third + sixth:
        for copy in copies:
            copy.wait_send()


def fused(
    wide,
    deep,
    inputs,
    attn_gain,
    w_query,
    w_key,
    w_value,
    w_out,
    ffn_gain,
    w_gate,
    w_up,
    w_down,
    key_cache,
    value_cache,
    lengths,
    positions,
):
    steps, requests, depth = inputs.shape
    rows = steps * requests
    local_rows, kv_count, slots, _ = key_cache.shape
    own = steps * local_rows
    query_cols, key_cols = w_query.shape[1], w_key.shape[1]
    group = query_cols // key_cols
    part = w_gate.shape[1] // wide
    chunks = max(1, depth // 1024)
    tile = depth // chunks
    source = np.arange(rows).reshape(steps, wide, local_rows).transpose(1, 2, 0).reshape(-1)
    perm = np.zeros((rows, rows), np.float32)
    perm[np.arange(rows), source] = 1.0
    half_dim = HD // 2
    freqs = 500000.0 ** (-(np.arange(half_dim) * 2.0 / HD))
    freqs = jnp.asarray(np.concatenate([freqs, freqs])[None], jnp.float32)
    pieces = query_cols // (2 * key_cols)
    vmem = pl.BlockSpec(memory_space=pltpu.VMEM)
    smem = pl.BlockSpec(memory_space=pltpu.SMEM)
    hbm = pl.BlockSpec(memory_space=pl.ANY)
    bf16, f32 = jnp.bfloat16, jnp.float32
    dma = pltpu.SemaphoreType.DMA
    heads = local_rows * kv_count
    scratch = [
        pltpu.VMEM(inputs.shape, bf16),
        pltpu.VMEM((1, depth), f32),
        pltpu.VMEM((1, depth), f32),
        pltpu.VMEM((rows, rows), bf16),
        pltpu.VMEM((rows, rows), bf16),
        pltpu.VMEM((1, HD), f32),
        pltpu.VMEM((2, local_rows, steps * group, HD), f32),
        pltpu.VMEM((rows, depth), f32),
        pltpu.VMEM((depth, query_cols), bf16),
        pltpu.VMEM((2, depth, key_cols), bf16),
        pltpu.VMEM((query_cols, depth), bf16),
        pltpu.VMEM((wide, depth, part), bf16),
        pltpu.VMEM((wide, depth, part), bf16),
        pltpu.VMEM(key_cache.shape, bf16),
        pltpu.VMEM(value_cache.shape, bf16),
        pltpu.VMEM((pieces + 1, wide, own, 2 * key_cols), bf16),
        pltpu.VMEM((pieces + 1, wide, own, 2 * key_cols), bf16),
        pltpu.VMEM((wide, own, 128), f32),
        pltpu.VMEM((wide, own, 128), f32),
        pltpu.VMEM((heads, steps * group, HD), f32),
        pltpu.VMEM((heads, steps * group, HD), f32),
        pltpu.VMEM((heads, steps * group, HD), f32),
        pltpu.VMEM((local_rows, steps, query_cols), f32),
        pltpu.VMEM((wide, local_rows, steps, query_cols), bf16),
        pltpu.VMEM((deep, chunks, rows, tile), bf16),
        pltpu.VMEM((rows, depth), f32),
        pltpu.VMEM((wide, 2, rows, part), bf16),
        pltpu.VMEM((wide, 2, rows, part), bf16),
        pltpu.VMEM((wide, rows, 128), f32),
        pltpu.VMEM((wide, rows, part), bf16),
        pltpu.VMEM((deep, chunks, rows, tile), bf16),
        dma((pieces + 5,)),
        dma((6,)),
        dma((2, wide)),
        dma((wide,)),
        dma((pieces + 1, wide)),
        dma((pieces + 1, wide)),
        dma((wide,)),
        dma((wide,)),
        dma((local_rows, wide)),
        dma((local_rows, wide)),
        dma((chunks, deep)),
        dma((chunks, deep)),
        dma((wide,)),
        dma((wide,)),
        dma((wide,)),
        dma((wide,)),
        dma((wide,)),
        dma((wide,)),
        dma((chunks, deep)),
        dma((chunks, deep)),
    ]
    return pl.pallas_call(
        functools.partial(layer_kernel, wide, deep),
        out_shape=jax.ShapeDtypeStruct(inputs.shape, f32),
        in_specs=[smem] * 2 + [hbm] * 15,
        out_specs=vmem,
        scratch_shapes=scratch,
        compiler_params=pltpu.CompilerParams(
            collective_id=0, has_side_effects=True, vmem_limit_bytes=60 * 1024 * 1024
        ),
        name="layer",
    )(
        lengths,
        positions,
        inputs,
        attn_gain[None],
        ffn_gain[None],
        jnp.asarray(perm, bf16),
        jnp.asarray(perm.T, bf16),
        freqs,
        w_query,
        w_key,
        w_value,
        w_out,
        w_gate,
        w_up,
        w_down,
        key_cache,
        value_cache,
    ).astype(bf16)


def local(wide, deep, *arrays):
    inputs, w_query, w_gate = arrays[0], arrays[2], arrays[7]
    fits = (
        wide % 2 == 0
        and wide <= 8
        and inputs.shape[1] % 8 == 0
        and inputs.shape[0] * inputs.shape[1] <= 32
        and w_query.shape[1] == w_query.shape[0]
        and w_query.shape[1] % (2 * arrays[3].shape[1]) == 0
        and w_gate.shape[1] // 2 <= w_query.shape[0]
        and w_gate.shape[1] % (wide * 128) == 0
    )
    return fused(wide, deep, *arrays) if fits else plain(*arrays)


def solution(mesh):
    in_specs = (
        P(None, "groups", "width"),
        P("width"),
        P("width", "hidden"),
        P("width", "hidden"),
        P("width", "hidden"),
        P("hidden", "width"),
        P("width"),
        P("width", "hidden"),
        P("width", "hidden"),
        P("hidden", "width"),
        P(("groups", "width"), "hidden", None, None),
        P(("groups", "width"), "hidden", None, None),
        P(("groups", "width")),
        P(("groups", "width")),
    )
    out_specs = P(None, "groups", "width")
    step = functools.partial(local, mesh.shape["width"], mesh.shape["hidden"])
    return jax.shard_map(step, mesh=mesh, in_specs=in_specs, out_specs=out_specs, check_vma=False)
```

profile of v0, /device:TPU:0, one launch (start us, length us, event | category | flops | bytes accessed | tf_op | source)
XLA Modules:
  0.0 42.7 jit_solution(10478978749061559583)
XLA Ops:
  0.0 41.1 %layer.1 = f32[2,8,2048]{2,1,0:T(8,128)} custom-call(s32[2]{0:T(128)} %lengths.1, s32[2]{0:T(128)} %positions.1, bf16[2,8,2048]{2,1,0:T(8,128)(2,1)} %x_hbm.1, f32[1,2048]{1,0:T(1,128)} %bitcast.2, f32[1,2048]{1,0:T(1,128)} %bitcast.3, bf16[16,16]{1,0:T(8,128)(2,1)} %constant.7.clone.perm_hbm, bf16[16,16]{1,0:T(8,128)(2,1)} %constant.8.clone.unperm_hbm, ...), custom_call_target="tpu_custom_call" | custom-call | tf_op jit(solution)/shard_map/layer/pallas_call | solution.py:671
  41.1 1.5 %convert_element_type.3 = bf16[2,8,2048]{2,1,0:T(8,128)(2,1)} convert(f32[2,8,2048]{2,1,0:T(8,128)} %layer.1) | non-fusion elementwise | flops 32768 | bytes 196608 | tf_op jit(solution)/shard_map/convert_element_type | solution.py:699
where the time goes:
time: 42.8 us; the launch traced here: 42.7 us
  Pallas kernels  41.1 us (96%)
  other arithmetic  1.54 us (4%)
    pallas_call x1, Pallas kernels, fused(): pl.pallas_call(functools.partial(layer_kernel, wide, deep), out_shape=jax...  41.1 us
    convert_element_type x1, other arithmetic, fused(): return pl.pallas_call(functools.partial(layer_kernel, wide, deep), out_sh...  1.54 us

commit v1 on v0

v1 whole, which is shorter than its diff:
```python
import functools
import math

import jax
import jax.numpy as jnp
import numpy as np
from jax import lax
from jax.experimental import pallas as pl
from jax.experimental.pallas import tpu as pltpu
from jax.sharding import PartitionSpec as P

HD = 128


def rotary(vectors, places):
    half_dim = vectors.shape[-1] // 2
    freqs = 500000.0 ** (-(jnp.arange(half_dim, dtype=jnp.float32) * 2.0 / vectors.shape[-1]))
    angles = places.astype(jnp.float32)[:, None, None] * freqs
    cosine = jnp.cos(angles)
    sine_vals = jnp.sin(angles)
    first_half = vectors[..., :half_dim]
    second_half = vectors[..., half_dim:]
    return jnp.concatenate(
        [
            first_half * cosine - second_half * sine_vals,
            second_half * cosine + first_half * sine_vals,
        ],
        axis=-1,
    )


def attention(queries, keys, values, new_keys, new_values, lengths):
    rows, steps = queries.shape[:2]
    kv_count = keys.shape[1]
    grouped = queries.reshape(rows, steps, kv_count, -1, HD)
    scale = 1.0 / math.sqrt(HD)
    old = jnp.einsum("rskgd,rkcd->rksgc", grouped, keys, preferred_element_type=jnp.float32) * scale
    new = (
        jnp.einsum("rskgd,rtkd->rksgt", grouped, new_keys, preferred_element_type=jnp.float32)
        * scale
    )
    seen = jnp.arange(keys.shape[2], dtype=jnp.int32) < lengths[:, None]
    seen = seen[:, None, None, None, :]
    order = jnp.arange(steps)[None, :] <= jnp.arange(steps)[:, None]
    order = order[None, None, :, None, :]
    old = jnp.where(seen, old, -1e30)
    new = jnp.where(order, new, -1e30)
    highest = jnp.maximum(jnp.max(old, axis=-1, keepdims=True), jnp.max(new, axis=-1, keepdims=True))
    old = jnp.where(seen, jnp.exp(old - highest), 0.0)
    new = jnp.where(order, jnp.exp(new - highest), 0.0)
    total = jnp.sum(old, axis=-1, keepdims=True) + jnp.sum(new, axis=-1, keepdims=True)
    old = (old / total).astype(jnp.bfloat16)
    new = (new / total).astype(jnp.bfloat16)
    mixed = jnp.einsum("rksgc,rkcd->rskgd", old, values, preferred_element_type=jnp.float32)
    mixed += jnp.einsum("rksgt,rtkd->rskgd", new, new_values, preferred_element_type=jnp.float32)
    return mixed.astype(jnp.bfloat16).reshape(rows, steps, -1)


def plain(
    inputs,
    attn_gain,
    w_query,
    w_key,
    w_value,
    w_out,
    ffn_gain,
    w_gate,
    w_up,
    w_down,
    key_cache,
    value_cache,
    lengths,
    positions,
):
    local_rows = key_cache.shape[0]
    steps, requests, depth = inputs.shape
    width = requests // local_rows * depth
    query_cols = w_query.shape[1]
    key_cols = w_key.shape[1]
    hidden_cols = w_gate.shape[1]
    rows = requests * steps
    current = inputs.transpose(1, 0, 2).reshape(rows, depth).astype(jnp.float32)
    squares = jnp.sum(current * current, axis=1, keepdims=True)
    scaled = (current * attn_gain).astype(jnp.bfloat16)
    joined = lax.psum_scatter(
        jnp.concatenate(
            [
                jnp.dot(scaled, w_query, preferred_element_type=jnp.float32),
                jnp.dot(scaled, w_key, preferred_element_type=jnp.float32),
                jnp.dot(scaled, w_value, preferred_element_type=jnp.float32),
                jnp.broadcast_to(squares, (rows, 128)),
            ],
            axis=1,
        ),
        "width",
        scatter_dimension=0,
        tiled=True,
    )
    inverse = lax.rsqrt(joined[:, -1:] / width + 1e-05)
    joined = joined * inverse
    shape = (local_rows * steps, -1, HD)
    places = (positions[:, None] + jnp.arange(steps, dtype=jnp.int32)).reshape(-1)
    turned = rotary(joined[:, : query_cols + key_cols].reshape(shape), places).astype(jnp.bfloat16)
    queries = turned[:, : query_cols // HD].reshape(local_rows, steps, -1, HD)
    new_keys = turned[:, query_cols // HD :].reshape(local_rows, steps, -1, HD)
    new_values = joined[:, query_cols + key_cols : query_cols + 2 * key_cols]
    new_values = new_values.astype(jnp.bfloat16).reshape(local_rows, steps, -1, HD)
    mixed = attention(queries, key_cache, value_cache, new_keys, new_values, lengths)
    attn_part = jnp.dot(
        lax.all_gather(mixed.reshape(local_rows * steps, -1), "width", axis=0, tiled=True),
        w_out,
        preferred_element_type=jnp.float32,
    )
    residual = current + lax.psum(attn_part, "hidden")
    res_squares = jnp.sum(residual * residual, axis=1, keepdims=True)
    ffn_in = (residual * ffn_gain).astype(jnp.bfloat16)
    both = lax.psum(
        jnp.concatenate(
            [
                jnp.dot(ffn_in, w_gate, preferred_element_type=jnp.float32),
                jnp.dot(ffn_in, w_up, preferred_element_type=jnp.float32),
                jnp.broadcast_to(res_squares, (rows, 128)),
            ],
            axis=1,
        ),
        "width",
    )
    summed = both * lax.rsqrt(both[:, -1:] / width + 1e-05)
    activated = (
        jax.nn.silu(summed[:, :hidden_cols]) * summed[:, hidden_cols : 2 * hidden_cols]
    ).astype(jnp.bfloat16)
    down_part = jnp.dot(activated, w_down, preferred_element_type=jnp.float32)
    total = lax.psum(down_part, "hidden")
    out = (residual + total).astype(jnp.bfloat16)
    return out.reshape(requests, steps, depth).transpose(1, 0, 2)


MESH = pl.DeviceIdType.MESH
TILE = 512


def far_first(place, n):
    half = n // 2
    flip = lax.div(place, half)
    near = place + flip * (n - 1 - 2 * place)
    alone = n - 1 - 2 * near
    order = []
    for i in range(n - 1):
        j = jnp.maximum(i - alone, 0)
        gap = near - lax.div(j, 2)
        other = jnp.where(i < alone, n - 1 - i, near + gap * (1 - 2 * lax.rem(j, 2)))
        order.append(other + flip * (n - 1 - 2 * other))
    return order


def layer_kernel(
    wide,
    deep,
    lengths_hbm,
    positions_hbm,
    x_hbm,
    attn_gain_hbm,
    ffn_gain_hbm,
    perm_hbm,
    unperm_hbm,
    freqs_hbm,
    w_query,
    w_key,
    w_value,
    w_out,
    w_gate,
    w_up,
    w_down,
    key_cache,
    value_cache,
    out_ref,
    lengths,
    positions,
    x_ref,
    attn_gain,
    ffn_gain,
    perm,
    unperm,
    freqs,
    angle_buf,
    down_buf,
    wq_buf,
    wkv_buf,
    wo_buf,
    wgu_buf,
    kc_buf,
    vc_buf,
    send1,
    recv1,
    ss_send1,
    ss_recv1,
    q_buf,
    k_buf,
    v_buf,
    mix_buf,
    gather,
    out_acc,
    red1,
    res_buf,
    gu_acc,
    send3,
    recv3,
    ss2,
    act_buf,
    red2,
    load_sem,
    small_sem,
    big_sem,
    down_sem,
    s1,
    r1,
    t1,
    u1,
    s2,
    r2,
    s3,
    r3,
    s4,
    r4,
    t4,
    u4,
    s5,
    r5,
    s6,
    r6,
):
    f32, bf16 = jnp.float32, jnp.bfloat16
    col = lax.axis_index("width")
    hid = lax.axis_index("hidden")
    steps, requests, depth = x_ref.shape
    rows = steps * requests
    local_rows, kv_count, slots, _ = kc_buf.shape
    own = steps * local_rows
    query_cols = wq_buf.shape[1]
    key_cols = w_key.shape[1]
    group = query_cols // key_cols
    head_cols = group * HD
    part = act_buf.shape[2]
    pair = 2 * part
    chunks = depth // TILE
    ends, end = red2.shape[1], red2.shape[3]
    width = wide * depth
    far = far_first(col, wide)

    def peer(base, k, n):
        return lax.rem(base + k, n)

    def dot(a, b):
        return jnp.dot(a, b, preferred_element_type=f32)

    sent = []

    def post(src, dst, send_sem, recv_sem, axis, to):
        copy = pltpu.make_async_remote_copy(
            src_ref=src,
            dst_ref=dst,
            send_sem=send_sem,
            recv_sem=recv_sem,
            device_id={axis: to},
            device_id_type=MESH,
        )
        copy.start()
        sent.append(copy)

    def take(dst, send_sem, recv_sem, axis, source):
        pltpu.make_async_remote_copy(
            src_ref=dst,
            dst_ref=dst,
            send_sem=send_sem,
            recv_sem=recv_sem,
            device_id={axis: source},
            device_id_type=MESH,
        ).wait_recv()

    barrier = pltpu.get_barrier_semaphore()
    for k in range(1, wide):
        pl.semaphore_signal(
            barrier, inc=1, device_id={"width": peer(col, k, wide)}, device_id_type=MESH
        )
    for k in range(1, deep):
        pl.semaphore_signal(
            barrier, inc=1, device_id={"hidden": peer(hid, k, deep)}, device_id_type=MESH
        )

    smalls = [
        pltpu.make_async_copy(src, dst, small_sem.at[i])
        for i, (src, dst) in enumerate(
            (
                (x_hbm, x_ref),
                (perm_hbm, perm),
                (attn_gain_hbm, attn_gain),
                (freqs_hbm, freqs),
                (unperm_hbm, unperm),
                (ffn_gain_hbm, ffn_gain),
                (lengths_hbm, lengths),
                (positions_hbm, positions),
            )
        )
    ]
    for load in smalls:
        load.start()
    loads = [
        pltpu.make_async_copy(w_key, wkv_buf.at[0], load_sem.at[0]),
        pltpu.make_async_copy(w_value, wkv_buf.at[1], load_sem.at[1]),
    ]
    pieces = send1.shape[0] - 1
    q_tile = query_cols // pieces
    for c in range(pieces):
        at = pl.ds(c * q_tile, q_tile)
        loads.append(
            pltpu.make_async_copy(w_query.at[:, at], wq_buf.at[:, at], load_sem.at[2 + c])
        )
    key_load = pltpu.make_async_copy(key_cache, kc_buf, load_sem.at[2 + pieces])
    value_load = pltpu.make_async_copy(value_cache, vc_buf, load_sem.at[3 + pieces])
    out_load = pltpu.make_async_copy(w_out, wo_buf, load_sem.at[4 + pieces])
    for load in loads:
        load.start()

    passes = [(0, 1), (1, chunks)] if chunks > 1 else [(0, chunks)]
    slots_of = far + [col]
    big = []
    for n, (lo, hi) in enumerate(passes):
        down = pl.ds(lo * TILE, (hi - lo) * TILE)
        big.append([])
        for i, p in enumerate(slots_of):
            at = pl.ds(pl.multiple_of(p * part, 128), part)
            for m, weight in enumerate((w_gate, w_up)):
                big[n].append(
                    pltpu.make_async_copy(
                        weight.at[down, at],
                        wgu_buf.at[down, pl.ds(i * pair + m * part, part)],
                        big_sem.at[n, i, m],
                    )
                )
    sources = [col] + far[::-1]
    down_loads = []
    for i, p in enumerate(sources):
        at = pl.ds(pl.multiple_of(p * part, 128), part)
        home = wq_buf if i < wide // 2 else wo_buf
        first_row = i % (wide // 2) * part
        down_loads.append(
            (
                pltpu.make_async_copy(
                    w_down.at[at], home.at[pl.ds(first_row, part)], down_sem.at[i]
                ),
                home,
                first_row,
            )
        )

    for load in smalls[:3]:
        load.wait()
    x_bf = jnp.concatenate([x_ref[s].astype(f32) for s in range(steps)], axis=0)
    turned = dot(perm[...], x_bf.astype(bf16))
    squares = jnp.sum(turned * turned, axis=1, keepdims=True)
    squares = jnp.broadcast_to(squares, (rows, 128))
    scaled = (turned * attn_gain[...]).astype(bf16)
    for w in range(wide):
        ss_send1[w] = squares[w * own : (w + 1) * own]

    def put(value, piece):
        value = value.astype(bf16)
        for w in range(wide):
            send1[piece, w] = value[w * own : (w + 1) * own]

    def ship(src, dst, a, b):
        for i, to in enumerate(far):
            post(src.at[to], dst.at[col], a.at[i], b.at[col], "width", to)

    loads[0].wait()
    loads[1].wait()
    put(jnp.concatenate([dot(scaled, wkv_buf[0]), dot(scaled, wkv_buf[1])], axis=1), 0)
    pl.semaphore_wait(barrier, wide + deep - 2)
    ship(ss_send1, ss_recv1, t1, u1)
    ship(send1.at[0], recv1.at[0], s1.at[0], r1.at[0])
    for c in range(pieces):
        loads[2 + c].wait()
        if c == 0:
            key_load.start()
            value_load.start()
        if c == min(1, pieces - 1):
            out_load.start()
        put(dot(scaled, wq_buf[:, c * q_tile : (c + 1) * q_tile]), c + 1)
        ship(send1.at[c + 1], recv1.at[c + 1], s1.at[c + 1], r1.at[c + 1])
        if c == min(2, pieces - 1):
            for load in big[0]:
                load.start()
    for batch in big[1:]:
        for load in batch:
            load.start()
    smalls[3].wait()
    smalls[7].wait()
    for r in range(local_rows):
        for s in range(steps):
            place = (positions[r] + s).astype(f32)
            angle_buf[0, r, s * group : (s + 1) * group, :] = jnp.broadcast_to(
                place * freqs[...], (group, HD)
            )
    lower_half = lax.broadcasted_iota(jnp.int32, (steps * group, HD), 1) < HD // 2
    for r in range(local_rows):
        angle = angle_buf[0, r]
        sin = jnp.sin(angle)
        angle_buf[0, r] = jnp.cos(angle)
        angle_buf[1, r] = jnp.where(lower_half, -sin, sin)

    smalls[6].wait()
    for i, p in enumerate(far):
        take(ss_recv1.at[p], t1.at[i], u1.at[p], "width", p)
    sums = ss_send1[col]
    for p in far:
        sums += ss_recv1[p]
    inverse = lax.rsqrt(sums[:, :1] / width + 1e-05)

    def whole(piece):
        for i, p in enumerate(far):
            take(recv1.at[piece, p], s1.at[piece, i], r1.at[piece, p], "width", p)
        value = send1[piece, col].astype(f32)
        for p in far:
            value += recv1[piece, p].astype(f32)
        return value * inverse

    fresh_kv = whole(0)
    totals = {}
    scale = 1.0 / math.sqrt(HD)
    step_of = lax.broadcasted_iota(jnp.int32, (steps * group, 1), 0)
    slot = lax.broadcasted_iota(jnp.int32, (steps * group, slots), 1)
    for h in range(kv_count):
        needed = range(h * head_cols // q_tile, ((h + 1) * head_cols - 1) // q_tile + 1)
        for piece in needed:
            if piece not in totals:
                totals[piece] = whole(piece + 1)
        for r in range(local_rows):
            for s in range(steps):
                row = r * steps + s
                for g in range(group):
                    at = (h * group + g) * HD
                    line = totals[at // q_tile][row : row + 1]
                    at %= q_tile
                    q_buf[r * kv_count + h, s * group + g : s * group + g + 1, :] = line[
                        :, at : at + HD
                    ]
                line = fresh_kv[row : row + 1]
                at = h * HD
                k_buf[r * kv_count + h, s * group : (s + 1) * group, :] = jnp.broadcast_to(
                    line[:, at : at + HD], (group, HD)
                )
                at += key_cols
                v_buf[r * kv_count + h, s * group : (s + 1) * group, :] = jnp.broadcast_to(
                    line[:, at : at + HD], (group, HD)
                )
        if h == 0:
            key_load.wait()
            value_load.wait()
        asked = []
        for r in range(local_rows):
            cos, sin = angle_buf[0, r], angle_buf[1, r]
            q = q_buf[r * kv_count + h]
            q = (q * cos + pltpu.roll(q, HD // 2, 1) * sin).astype(bf16)
            scores = lax.dot_general(
                q, kc_buf[r, h], (((1,), (1,)), ((), ())), preferred_element_type=f32
            )
            asked.append((q.astype(f32), cos, sin, scores))
        weighed = []
        for r, (q, cos, sin, scores) in enumerate(asked):
            seen = slot < lengths[r]
            nk = k_buf[r * kv_count + h]
            nk = (nk * cos + pltpu.roll(nk, HD // 2, 1) * sin).astype(bf16).astype(f32)
            scores = jnp.where(seen, scores * scale, -1e30)
            highest = jnp.max(scores, axis=1, keepdims=True)
            fresh = []
            for s in range(steps):
                new = jnp.sum(q * nk[s * group : s * group + 1], axis=1, keepdims=True)
                new = jnp.where(step_of >= s * group, new * scale, -1e30)
                fresh.append(new)
                highest = jnp.maximum(highest, new)
            weights = jnp.where(seen, jnp.exp(scores - highest), 0.0)
            for s in range(steps):
                fresh[s] = jnp.where(step_of >= s * group, jnp.exp(fresh[s] - highest), 0.0)
            weighed.append((weights, fresh))
        blends = [
            dot(weights.astype(bf16), vc_buf[r, h]) for r, (weights, _) in enumerate(weighed)
        ]
        for r, (weights, fresh) in enumerate(weighed):
            nv = v_buf[r * kv_count + h].astype(bf16).astype(f32)
            norm = jnp.sum(weights, axis=1, keepdims=True)
            mixed = blends[r]
            for s in range(steps):
                norm += fresh[s]
                mixed += fresh[s].astype(bf16).astype(f32) * nv[s * group : s * group + 1]
            mixed = mixed * (1.0 / norm)
            for s in range(steps):
                row = r * steps + s
                for g in range(group):
                    mix_buf[h, row : row + 1, g * HD : (g + 1) * HD] = mixed[
                        s * group + g : s * group + g + 1
                    ]
        gather[h, col] = mix_buf[h].astype(bf16)
        for i, to in enumerate(far):
            post(gather.at[h, col], gather.at[h, col], s2.at[h, i], r2.at[h, col], "width", to)
    for load in smalls[4:6]:
        load.wait()

    def spread(red, c, a, b):
        for k in range(deep - 1, 0, -1):
            to = peer(hid, k, deep)
            post(red.at[hid, c], red.at[hid, c], a.at[c, k], b.at[c, hid], "hidden", to)

    def reduced(red, c, a, b):
        for k in range(1, deep):
            p = peer(hid, k, deep)
            take(red.at[p, c], a.at[c, k], b.at[c, p], "hidden", p)
        value = red[0, c].astype(f32)
        for i in range(1, deep):
            value += red[i, c].astype(f32)
        return value

    for h in range(kv_count):
        for i, p in enumerate(far[::-1]):
            take(gather.at[h, p], s2.at[h, wide - 2 - i], r2.at[h, p], "width", p)
        mixed = jnp.concatenate([gather[h, w].astype(f32) for w in range(wide)], axis=0)
        mixed = dot(unperm[...], mixed.astype(bf16)).astype(bf16)
        if h == 0:
            out_load.wait()
        for c in range(chunks):
            at = slice(c * TILE, (c + 1) * TILE)
            value = dot(mixed, wo_buf[h * head_cols : (h + 1) * head_cols, at])
            if h:
                value += out_acc[:, at]
            if h < kv_count - 1:
                out_acc[:, at] = value
            else:
                red1[hid, c] = value.astype(bf16)
                spread(red1, c, s3, r3)
    for load, _, _ in down_loads:
        load.start()

    res_squares = jnp.zeros((rows, 1), f32)
    for n, (lo, hi) in enumerate(passes):
        for c in range(lo, hi):
            at = slice(c * TILE, (c + 1) * TILE)
            value = reduced(red1, c, s3, r3)
            value += jnp.concatenate([x_ref[s, :, at].astype(f32) for s in range(steps)], axis=0)
            res_buf[:, at] = value
            res_squares += jnp.sum(value * value, axis=1, keepdims=True)
        last = n == len(passes) - 1
        if last:
            ss2[col] = jnp.broadcast_to(res_squares, (rows, 128))
            for i, to in enumerate(far):
                post(ss2.at[col], ss2.at[col], t4.at[i], u4.at[col], "width", to)
        deep_at = slice(lo * TILE, hi * TILE)
        ffn_in = (res_buf[:, deep_at] * ffn_gain[:, deep_at]).astype(bf16)
        for load in big[n]:
            load.wait()
        shipped = 0
        for c in range(wide * pair // TILE):
            at = slice(c * TILE, (c + 1) * TILE)
            value = dot(ffn_in, wgu_buf[deep_at, at])
            if n:
                value += gu_acc[:, at]
            if not last:
                gu_acc[:, at] = value
                continue
            send3[:, at] = value.astype(bf16)
            while shipped < 2 * (wide - 1) and (shipped + 1) * part <= (c + 1) * TILE:
                i, m = shipped // 2, shipped % 2
                mine = send3.at[:, pl.ds(shipped * part, part)]
                post(mine, recv3.at[col, m], s4.at[i, m], r4.at[col, m], "width", far[i])
                shipped += 1
    at = (wide - 1) * pair
    gate = send3[:, at : at + part].astype(f32)
    up = send3[:, at + part : at + pair].astype(f32)
    sums = ss2[col]
    for i, p in enumerate(far):
        take(ss2.at[p], t4.at[i], u4.at[p], "width", p)
        sums += ss2[p]
    inverse = lax.rsqrt(sums[:, :1] / width + 1e-05)
    for i, p in enumerate(far):
        for m in range(2):
            take(recv3.at[p, m], s4.at[i, m], r4.at[p, m], "width", p)
    for p in far:
        gate += recv3[p, 0].astype(f32)
        up += recv3[p, 1].astype(f32)
    gate, up = gate * inverse, up * inverse
    act_buf[col] = (gate / (1.0 + jnp.exp(-gate)) * up).astype(bf16)
    for i, to in enumerate(far):
        post(act_buf.at[col], act_buf.at[col], s5.at[i], r5.at[col], "width", to)
    for i, p in enumerate(sources):
        if i:
            take(act_buf.at[p], s5.at[wide - 1 - i], r5.at[p], "width", p)
        load, home, first_row = down_loads[i]
        load.wait()
        act = act_buf[p]
        for c in range(ends):
            at = slice(c * end, (c + 1) * end)
            value = dot(act, home[first_row : first_row + part, at])
            if i:
                value += down_buf[:, at]
            if i < wide - 1:
                down_buf[:, at] = value
            else:
                red2[hid, c] = value.astype(bf16)
                spread(red2, c, s6, r6)
    for c in range(ends):
        at = slice(c * end, (c + 1) * end)
        value = res_buf[:, at] + reduced(red2, c, s6, r6)
        for s in range(steps):
            out_ref[s, :, at] = value[s * requests : (s + 1) * requests]
    for copy in sent:
        copy.wait_send()


def fused(
    wide,
    deep,
    inputs,
    attn_gain,
    w_query,
    w_key,
    w_value,
    w_out,
    ffn_gain,
    w_gate,
    w_up,
    w_down,
    key_cache,
    value_cache,
    lengths,
    positions,
):
    steps, requests, depth = inputs.shape
    rows = steps * requests
    local_rows, kv_count, slots, _ = key_cache.shape
    own = steps * local_rows
    query_cols, key_cols = w_query.shape[1], w_key.shape[1]
    group = query_cols // key_cols
    part = w_gate.shape[1] // wide
    chunks = depth // TILE
    ends = max(1, chunks // 2)
    source = np.arange(rows).reshape(steps, wide, local_rows).transpose(1, 2, 0).reshape(-1)
    perm = np.zeros((rows, rows), np.float32)
    perm[np.arange(rows), source] = 1.0
    half_dim = HD // 2
    freqs = 500000.0 ** (-(np.arange(half_dim) * 2.0 / HD))
    freqs = jnp.asarray(np.concatenate([freqs, freqs])[None], jnp.float32)
    pieces = query_cols // (2 * key_cols)
    hbm = pl.BlockSpec(memory_space=pl.ANY)
    bf16, f32 = jnp.bfloat16, jnp.float32
    dma = pltpu.SemaphoreType.DMA
    heads = local_rows * kv_count
    scratch = [
        pltpu.SMEM(lengths.shape, jnp.int32),
        pltpu.SMEM(positions.shape, jnp.int32),
        pltpu.VMEM(inputs.shape, bf16),
        pltpu.VMEM((1, depth), f32),
        pltpu.VMEM((1, depth), f32),
        pltpu.VMEM((rows, rows), bf16),
        pltpu.VMEM((rows, rows), bf16),
        pltpu.VMEM((1, HD), f32),
        pltpu.VMEM((2, local_rows, steps * group, HD), f32),
        pltpu.VMEM((rows, depth), f32),
        pltpu.VMEM((depth, query_cols), bf16),
        pltpu.VMEM((2, depth, key_cols), bf16),
        pltpu.VMEM((query_cols, depth), bf16),
        pltpu.VMEM((depth, wide * 2 * part), bf16),
        pltpu.VMEM(key_cache.shape, bf16),
        pltpu.VMEM(value_cache.shape, bf16),
        pltpu.VMEM((pieces + 1, wide, own, 2 * key_cols), bf16),
        pltpu.VMEM((pieces + 1, wide, own, 2 * key_cols), bf16),
        pltpu.VMEM((wide, own, 128), f32),
        pltpu.VMEM((wide, own, 128), f32),
        pltpu.VMEM((heads, steps * group, HD), f32),
        pltpu.VMEM((heads, steps * group, HD), f32),
        pltpu.VMEM((heads, steps * group, HD), f32),
        pltpu.VMEM((kv_count, own, group * HD), f32),
        pltpu.VMEM((kv_count, wide, own, group * HD), bf16),
        pltpu.VMEM((rows, depth), f32),
        pltpu.VMEM((deep, chunks, rows, TILE), bf16),
        pltpu.VMEM((rows, depth), f32),
        pltpu.VMEM((rows, wide * 2 * part), f32),
        pltpu.VMEM((rows, wide * 2 * part), bf16),
        pltpu.VMEM((wide, 2, rows, part), bf16),
        pltpu.VMEM((wide, rows, 128), f32),
        pltpu.VMEM((wide, rows, part), bf16),
        pltpu.VMEM((deep, ends, rows, depth // ends), bf16),
        dma((pieces + 5,)),
        dma((8,)),
        dma((2, wide, 2)),
        dma((wide,)),
        dma((pieces + 1, wide)),
        dma((pieces + 1, wide)),
        dma((wide,)),
        dma((wide,)),
        dma((kv_count, wide)),
        dma((kv_count, wide)),
        dma((chunks, deep)),
        dma((chunks, deep)),
        dma((wide, 2)),
        dma((wide, 2)),
        dma((wide,)),
        dma((wide,)),
        dma((wide,)),
        dma((wide,)),
        dma((ends, deep)),
        dma((ends, deep)),
    ]
    return pl.pallas_call(
        functools.partial(layer_kernel, wide, deep),
        out_shape=pltpu.VMEM(inputs.shape, f32),
        in_specs=[hbm] * 17,
        out_specs=pl.BlockSpec(memory_space=pltpu.VMEM),
        scratch_shapes=scratch,
        compiler_params=pltpu.CompilerParams(
            collective_id=0, has_side_effects=True, vmem_limit_bytes=56 * 1024 * 1024
        ),
        name="layer",
    )(
        lengths,
        positions,
        inputs,
        attn_gain[None],
        ffn_gain[None],
        jnp.asarray(perm, bf16),
        jnp.asarray(perm.T, bf16),
        freqs,
        w_query,
        w_key,
        w_value,
        w_out,
        w_gate,
        w_up,
        w_down,
        key_cache,
        value_cache,
    ).astype(bf16)


def local(wide, deep, *arrays):
    inputs, w_query, w_gate = arrays[0], arrays[2], arrays[7]
    fits = (
        wide % 2 == 0
        and wide <= 8
        and inputs.shape[1] % 8 == 0
        and inputs.shape[0] * inputs.shape[1] <= 32
        and w_query.shape[1] == w_query.shape[0]
        and w_query.shape[1] % (2 * arrays[3].shape[1]) == 0
        and w_gate.shape[1] // 2 <= w_query.shape[0]
        and w_gate.shape[1] % (wide * 128) == 0
        and w_gate.shape[1] * 2 % TILE == 0
        and w_query.shape[0] % (2 * TILE) == 0
    )
    return fused(wide, deep, *arrays) if fits else plain(*arrays)


def solution(mesh):
    in_specs = (
        P(None, "groups", "width"),
        P("width"),
        P("width", "hidden"),
        P("width", "hidden"),
        P("width", "hidden"),
        P("hidden", "width"),
        P("width"),
        P("width", "hidden"),
        P("width", "hidden"),
        P("hidden", "width"),
        P(("groups", "width"), "hidden", None, None),
        P(("groups", "width"), "hidden", None, None),
        P(("groups", "width")),
        P(("groups", "width")),
    )
    out_specs = P(None, "groups", "width")
    step = functools.partial(local, mesh.shape["width"], mesh.shape["hidden"])
    return jax.shard_map(step, mesh=mesh, in_specs=in_specs, out_specs=out_specs, check_vma=False)
```

time: 42.8 us -> 38.4 us (0.90)
  Pallas kernels: 41.1 us -> 37.6 us
  other arithmetic: 1.54 us -> 0.64 us
    pallas_call x1, Pallas kernels: 41.1 us -> 37.6 us  [fused(): pl.pallas_call(functools.partial(layer_kernel, wide, deep), out_shape=plt...]
    convert_element_type x1, other arithmetic: 1.54 us -> 0.64 us  [fused(): return pl.pallas_call(functools.partial(layer_kernel, wide, deep), out_sh...]
where the time goes in v1:
time: 38.4 us; the launch traced here: 38.2 us
  Pallas kernels  37.6 us (98%)
  other arithmetic  0.64 us (2%)
    pallas_call x1, Pallas kernels, fused(): pl.pallas_call(functools.partial(layer_kernel, wide, deep), out_shape=plt...  37.6 us

profile of v1, /device:TPU:0, one launch (start us, length us, event | category | flops | bytes accessed | tf_op | source)
XLA Modules:
  0.0 38.2 jit_solution(4107091243109148758)
XLA Ops:
  0.0 37.6 %layer.1 = f32[2,8,2048]{2,1,0:T(8,128)S(1)} custom-call(s32[2]{0:T(128)} %lengths_hbm.1, s32[2]{0:T(128)} %positions_hbm.1, bf16[2,8,2048]{2,1,0:T(8,128)(2,1)} %x_hbm.1, f32[1,2048]{1,0:T(1,128)} %bitcast.2, f32[1,2048]{1,0:T(1,128)} %bitcast.3, bf16[16,16]{1,0:T(8,128)(2,1)} %constant.7.clone.perm_hbm, bf16[16,16]{1,0:T(8,128)(2,1)} %constant.8.clone.unperm_hbm, ...), custom_call_target="tpu_custom_call" | custom-call | tf_op jit(solution)/shard_map/layer/pallas_call | solution.py:711
  37.6 0.6 %convert_element_type.3 = bf16[2,8,2048]{2,1,0:T(8,128)(2,1)} convert(f32[2,8,2048]{2,1,0:T(8,128)S(1)} %layer.1) | non-fusion elementwise | flops 32768 | bytes 196608 | tf_op jit(solution)/shard_map/convert_element_type | solution.py:739
